TPU v7x, 512 devices: a whole 4x4x16 slice. The times are simulated.
512 devices in a mesh: dp: 8 (over y, core), expert: 64 (over x, z).
Axes of the slice: x: 4, y: 4, z: 16, core: 2. Of those that a mesh axis runs over, the one named last changes fastest.
Arguments:
- grad_out: bfloat16 [32768, 4096], P('expert', 'dp'), may hold values from -30 to 30
- hidden: bfloat16 [32768, 2, 1024], P('expert', None, 'dp'), may hold values from -24 to 24
- gate_prob: float32 [32768, 2], P('expert'), may hold values from 0.05 to 1
- expert_ids: int32 [32768, 2], P('expert'), may hold values from 0 to 63, all different within a row; in each aligned block of 512 rows (0 to 511, 512 to 1023, ...) at most 20 rows name the same one
- weights: bfloat16 [64, 1024, 4096], P('expert', None, 'dp'), may hold values from -0.1875 to 0.1875
Outputs:
- hidden_grad: bfloat16 [32768, 2, 1024], P('expert', None, 'dp')
- update: float32 [64, 1024, 4096], P('expert', None, 'dp')
Inputs may be any that keep to these rules, and one draw needn't show every extreme that they name: `expert_ids`: among the 512 tokens of one index of expert, no expert is named by more than 20 choices, a bound that some block reaches; the 2 experts of a token differ.
All inputs are finite; a program needn't handle non-finite values.
Results may differ from a plain program's by a relative error of at most 0.019.
Values may be sent and summed in bfloat16 or wider, within the bound.
No kernel may reach another device: no remote copies, remote signals or barrier semaphores. Data moves between devices by JAX's collectives and lax.ppermute only.
A program may use at most 64 MiB of HBM per device.

v0:
```python
import jax
import jax.numpy as jnp
from jax import lax
from jax.sharding import PartitionSpec as P

D = 4096


def slot_numbers(route_ids, capacity, expert_count):
    flat_ids = route_ids.reshape(-1)
    one_hot = (flat_ids[:, None] == jnp.arange(expert_count, dtype=jnp.int32)[None, :]).astype(
        jnp.int32
    )
    before = jnp.cumsum(one_hot, axis=0) - one_hot
    rank_in = jnp.sum(before * one_hot, axis=1)
    return flat_ids * capacity + rank_in


def gram_sum(matrix_part):
    partial_gram = jnp.dot(matrix_part, matrix_part.T, preferred_element_type=jnp.float32)
    return lax.psum(partial_gram.astype(jnp.bfloat16), "dp").astype(jnp.float32)


def place_slots(slot_index, values, slot_count):
    empty_rows = jnp.zeros((slot_count,) + values.shape[1:], values.dtype)
    return empty_rows.at[slot_index].set(values)


def per_device(grad_out, hidden, gate_prob, expert_ids, weights):
    tokens, width_part = grad_out.shape
    top_count = expert_ids.shape[1]
    experts = lax.axis_size("expert")
    capacity = 5 * tokens * top_count // (4 * experts)
    total_slots = experts * capacity
    pair_count = tokens * top_count
    slot_index = slot_numbers(expert_ids, capacity, experts)
    token_of = jnp.arange(pair_count, dtype=jnp.int32) // top_count
    send_grad = place_slots(slot_index, grad_out[token_of], total_slots).reshape(
        experts, capacity, width_part
    )
    scaled_part = (gate_prob[:, :, None] * hidden.astype(jnp.float32)).astype(jnp.bfloat16)
    whole_scaled = lax.all_gather(scaled_part, "dp", axis=2, tiled=True)
    send_scaled = place_slots(
        slot_index, whole_scaled.reshape(pair_count, -1), total_slots
    ).reshape(experts, capacity, -1)
    got_grad, got_scaled = (
        lax.all_to_all(send_grad, "expert", split_axis=0, concat_axis=0, tiled=True),
        lax.all_to_all(send_scaled, "expert", split_axis=0, concat_axis=0, tiled=True),
    )
    got_grad = got_grad.reshape(total_slots, width_part)
    got_scaled = got_scaled.reshape(total_slots, -1)
    weight_part = weights[0]
    gradient = lax.dot_general(
        got_scaled, got_grad, (((0,), (0,)), ((), ())), preferred_element_type=jnp.float32
    )
    back_term = lax.dot_general(
        got_grad, weight_part, (((1,), (1,)), ((), ())), preferred_element_type=jnp.float32
    )
    flat_prob = gate_prob.reshape(-1)
    summed = lax.psum_scatter(
        back_term.astype(jnp.bfloat16), "dp", scatter_dimension=1, tiled=True
    ).astype(jnp.float32)
    returned = lax.all_to_all(
        summed.reshape(experts, capacity, -1).astype(jnp.bfloat16),
        "expert",
        split_axis=0,
        concat_axis=0,
        tiled=True,
    ).astype(jnp.float32)
    picked = returned.reshape(total_slots, -1)[slot_index]
    hidden_grad = (flat_prob[:, None] * picked).astype(jnp.bfloat16).reshape(tokens, top_count, -1)
    grad_bf16 = gradient.astype(jnp.bfloat16)
    gram_first = gram_sum(grad_bf16)
    norm_sq = jnp.sqrt(jnp.sum(gram_first * gram_first)) + 1e-06
    current = (grad_bf16.astype(jnp.float32) * lax.rsqrt(norm_sq)).astype(jnp.bfloat16)
    gram_now = (gram_first / norm_sq).astype(jnp.bfloat16)
    following = current.astype(jnp.float32)
    for sweep_number in range(2):
        if sweep_number > 0:
            gram_now = gram_sum(current).astype(jnp.bfloat16)
        following = 1.5 * current.astype(jnp.float32) - 0.5 * jnp.dot(
            gram_now, current, preferred_element_type=jnp.float32
        )
        current = following.astype(jnp.bfloat16)
    update = following * D**0.5
    return (hidden_grad, update[None])


def solution(mesh):
    in_specs = (
        P("expert", "dp"),
        P("expert", None, "dp"),
        P("expert", None),
        P("expert", None),
        P("expert", None, "dp"),
    )
    out_specs = (P("expert", None, "dp"), P("expert", None, "dp"))
    return jax.shard_map(
        per_device, mesh=mesh, in_specs=in_specs, out_specs=out_specs, check_vma=False
    )
```

profile of v0, /device:TPU:2, one launch (start us, length us, event | category | flops | bytes accessed | tf_op | source)
XLA Modules:
  0.0 626.0 jit_solution(6197987789082699378)
XLA Ops:
  7.2 0.8 broadcast_multiply_fusion
  8.0 0.8 copy.19
  9.6 18.0 %reduce-window.6 = s32[64,8,128]{2,1,0:T(8,128)S(1)} reduce-window(s32[64,8,128]{2,1,0:T(8,128)S(1)} %fusion.21, s32[]{:T(128)} %constant.16.clone.1), window={size=1x1x128 pad=0_0x0_0x127_0}, to_apply=%region_0.0 | reduce-window | flops 8323072 | bytes 524292 | tf_op jit(solution)/shard_map/reduce-window
  28.2 12.8 %scatter_custom_fusion = bf16[1280,512]{1,0:T(8,128)(2,1)S(1)} fusion(s32[1024]{0:T(1024)S(1)} %bitcast.46, bf16[512,512]{1,0:T(8,128)(2,1)} %param.5, s32[1024]{0:T(1024)S(1)} %broadcast_clamp_fusion.1, bf16[]{:T(256)} %constant.13.clone.1), kind=kCustom, calls=%fused_computation.22 | custom fusion | bytes 1311232 | tf_op jit(solution)/shard_map/scatter | solution.py:26
  41.0 1.3 reshape.124
  42.3 94.8 %all_to_all.15 = bf16[64,20,512]{2,1,0:T(8,128)(2,1)S(1)} all-to-all(bf16[64,20,512]{2,1,0:T(8,128)(2,1)} %reshape.124), channel_id=1, replica_groups=mesh['dp'=8,'expert'=64] {'expert'}, dimensions={0} | all-to-all | bytes 2621440 | tf_op jit(solution)/shard_map/all_to_all | solution.py:47
  137.1 1.2 reshape.125
  138.3 4.4 convolution_convert_fusion
  142.7 4.4 copy.25
  147.1 35.3 %reduce-scatter.4.cloned.1.call-done = bf16[128,1280]{1,0:T(8,128)(2,1)} async-done(((bf16[1024,1280]{1,0:T(8,128)(2,1)}), bf16[128,1280]{1,0:T(8,128)(2,1)}) %reduce-scatter.4.cloned.1.call-update) | async-done | bytes 327696
  182.4 1.2 copy.26
  183.5 0.8 convert_element_type.61
  184.4 15.8 %all-to-all-start.1 = ((bf16[64,20,128]{2,1,0:T(8,128)(2,1)}), bf16[64,20,128]{2,1,0:T(8,128)(2,1)}, u32[]{:S(2)}, u32[]{:S(2)}) async-start(bf16[64,20,128]{2,1,0:T(8,128)(2,1)} %convert_element_type.61), calls=%async_computation.1 | async-start | bytes 786432 | tf_op jit(solution)/shard_map/all_to_all | solution.py:63
  200.4 23.1 %all-to-all-done.1 = bf16[64,20,128]{2,1,0:T(8,128)(2,1)} async-done(((bf16[64,20,128]{2,1,0:T(8,128)(2,1)}), bf16[64,20,128]{2,1,0:T(8,128)(2,1)}, u32[]{:S(2)}, u32[]{:S(2)}) %all-to-all-start.1) | async-done | bytes 327712 | tf_op jit(solution)/shard_map/all_to_all | solution.py:63
  223.6 1.1 reshape.131
  224.6 4.0 gather_fusion
  228.7 2.4 multiply_convert_fusion.2
  231.4 35.5 %all-gather.2.cloned.1.call-done = bf16[512,2,1024]{2,1,0:T(2,128)(2,1)} async-done(((bf16[512,2,128]{2,1,0:T(2,128)(2,1)}), bf16[512,2,1024]{2,1,0:T(2,128)(2,1)}) %all-gather.2.cloned.1.call-update) | async-done | bytes 2097168 | tf_op jit(solution)/shard_map/all_gather | solution.py:42
  266.8 4.1 reshape.160
  270.9 7.8 %scatter_custom_fusion.1 = bf16[1280,1024]{1,0:T(8,128)(2,1)} fusion(s32[1024]{0:T(1024)S(1)} %bitcast.48, bf16[1024,1024]{1,0:T(8,128)(2,1)} %reshape.160, bf16[]{:T(256)} %constant.13.clone.1), kind=kCustom, calls=%fused_computation.19 | custom fusion | bytes 2621952 | tf_op jit(solution)/shard_map/scatter | solution.py:26
  278.7 5.2 reshape.129
  283.9 159.6 %all_to_all.16 = bf16[64,20,1024]{2,1,0:T(8,128)(2,1)S(1)} all-to-all(bf16[64,20,1024]{2,1,0:T(8,128)(2,1)} %reshape.129), channel_id=1, replica_groups=mesh['dp'=8,'expert'=64] {'expert'}, dimensions={0} | all-to-all | bytes 5242880 | tf_op jit(solution)/shard_map/all_to_all | solution.py:48
  443.5 2.9 bitcast_convert_fusion
  446.4 1.0 copy-done.3
  447.3 2.6 convolution_convert_fusion.2
  450.2 73.4 %all-reduce.3.cloned.1.call-done = bf16[1024,1024]{1,0:T(8,128)(2,1)} async-done(((bf16[1024,1024]{1,0:T(8,128)(2,1)}), bf16[1024,1024]{1,0:T(8,128)(2,1)}) %all-reduce.3.cloned.1.call-update) | async-done | bytes 2097168 | tf_op jit(solution)/shard_map/psum | solution.py:21
  523.6 3.4 fusion
  527.8 2.9 subtract_convert_fusion
  530.8 1.0 copy-done.4
  531.7 2.6 convolution_convert_fusion.1
  534.4 80.9 %all-reduce.5.cloned.1.call-done = bf16[1024,1024]{1,0:T(8,128)(2,1)} async-done(((bf16[1024,1024]{1,0:T(8,128)(2,1)}), bf16[1024,1024]{1,0:T(8,128)(2,1)}) %all-reduce.5.cloned.1.call-update) | async-done | bytes 2097168 | tf_op jit(solution)/shard_map/psum | solution.py:21
  615.2 4.2 multiply_bitcast_fusion
  (35 shorter events, 2.1 us)
Async XLA Ops:
  7.2 131.1 %copy-start = (bf16[1,1024,512]{2,1,0:T(8,128)(2,1)S(1)}, bf16[1,1024,512]{2,1,0:T(8,128)(2,1)}, u32[]{:S(2)}) copy-start(bf16[1,1024,512]{2,1,0:T(8,128)(2,1)} %param.9) | copy-start | bytes 3145732
  7.2 175.2 %reduce-scatter.4.cloned.1.call-start = ((), (), s32[]{:S(2)}) async-start(), calls=%async_computation.7 | async-start | bytes 2949120
  147.1 53.2 %copy-start.2 = (f32[512,2]{0,1:T(2,128)S(1)}, f32[512,2]{0,1:T(2,128)}, u32[]{:S(2)}) copy-start(f32[512,2]{0,1:T(2,128)} %param.7) | copy-start | bytes 12292
  184.4 39.2 %all-to-all-start.1 = ((bf16[64,20,128]{2,1,0:T(8,128)(2,1)}), bf16[64,20,128]{2,1,0:T(8,128)(2,1)}, u32[]{:S(2)}, u32[]{:S(2)}) async-start(bf16[64,20,128]{2,1,0:T(8,128)(2,1)} %convert_element_type.61), calls=%async_computation.1 | async-start | bytes 786432 | tf_op jit(solution)/shard_map/all_to_all | solution.py:63
  200.2 66.6 %all-gather.2.cloned.1.call-start = ((), (), s32[]{:S(2)}) async-start(), calls=%async_computation.4 | async-start | bytes 2359296 | tf_op jit(solution)/shard_map/all_gather | solution.py:42
  231.1 292.5 %all-reduce.3.cloned.1.call-start = ((), (), s32[]{:S(2)}) async-start(), calls=%async_computation.5 | async-start | bytes 4194304 | tf_op jit(solution)/shard_map/psum | solution.py:21
  446.4 1.0 copy-start.3
  450.0 165.3 %all-reduce.5.cloned.1.call-start = ((), (), s32[]{:S(2)}) async-start(), calls=%async_computation.6 | async-start | bytes 4194304 | tf_op jit(solution)/shard_map/psum | solution.py:21
  523.6 4.2 copy-start.1
  530.8 1.0 copy-start.4
  534.3 80.9 %copy-start.5 = (bf16[1024,512]{1,0:T(8,128)(2,1)S(1)}, bf16[1024,512]{1,0:T(8,128)(2,1)}, u32[]{:S(2)}) copy-start(bf16[1024,512]{1,0:T(8,128)(2,1)} %copy-done.4) | copy-start | bytes 3145732
Sparse Core Ops, SparseCore 0:
  147.2 35.1 reduce-scatter.3
  231.2 35.5 all-gather.1
  450.1 73.4 all-reduce.2
  534.5 80.7 all-reduce.4
where the time goes:
time: 627 us; the launch traced here: 626 us
  blocking collectives  254 us (41%)
  waiting for transfers between devices  248 us (40%)
  local copies, waits for them, and re-layouts  47.8 us (8%)
  other arithmetic  24.9 us (4%)
  matrix products  19.6 us (3%)
  starting transfers between devices  16.4 us (3%)
  between operations  14.7 us (2%)
    all_to_all x1, blocking collectives, per_device(): lax.all_to_all(send_scaled, 'expert', split_axis=0, concat_axis=0, tiled=...  160 us
    psum x2, waiting for transfers between devices, gram_sum(): return lax.psum(partial_gram.astype(jnp.bfloat16), 'dp').astype(jnp.float32)  154 us
    all_to_all x1, blocking collectives, per_device(): lax.all_to_all(send_grad, 'expert', split_axis=0, concat_axis=0, tiled=True)  94.8 us
    all_gather x1, waiting for transfers between devices, per_device(): whole_scaled = lax.all_gather(scaled_part, 'dp', axis=2, tiled=True)  35.5 us
    unnamed x5, waiting for transfers between devices  35.4 us
    all_to_all x1, waiting for transfers between devices, per_device(): lax.all_to_all(summed.reshape(experts, capacity, -1).astype(jnp.bfloat16)...  23.1 us
    scatter x2, local copies, waits for them, and re-layouts, place_slots(): return empty_rows.at[slot_index].set(values)  20.6 us
    another operation x3, other arithmetic  18.2 us
  transfers between devices with their start and end apart: 5, of which 5 were waited for; matrix products, arithmetic and copies ran while one was open for 0% of the time, Pallas kernels for 0%

commit v1 on v0

--- a/solution.py
+++ b/solution.py
@@ -39,7 +39,9 @@
         experts, capacity, width_part
     )
     scaled_part = (gate_prob[:, :, None] * hidden.astype(jnp.float32)).astype(jnp.bfloat16)
-    whole_scaled = lax.all_gather(scaled_part, "dp", axis=2, tiled=True)
+    whole_scaled = jnp.concatenate(
+        lax.all_to_all(jnp.stack([scaled_part] * lax.axis_size("dp")), "dp", 0, 0), axis=2
+    )
     send_scaled = place_slots(
         slot_index, whole_scaled.reshape(pair_count, -1), total_slots
     ).reshape(experts, capacity, -1)

time: 627 us -> 607 us (0.968)
  waiting for transfers between devices: 248 us -> 211 us
  blocking collectives: 254 us -> 277 us
    all_gather x1 -> x0, waiting for transfers between devices: 35.5 us -> none  [per_device(): whole_scaled = lax.all_gather(scaled_part, 'dp', axis=2, tiled=True)]
    all_to_all x0 -> x1, blocking collectives: none -> 31.3 us  [per_device(): lax.all_to_all(jnp.stack([scaled_part] * lax.axis_size('dp')), 'dp', 0, 0)]
    all_to_all x1, blocking collectives: 160 us -> 151 us  [per_device(): lax.all_to_all(send_scaled, 'expert', split_axis=0, concat_axis=0, tiled=...]
    unnamed x5 -> x4, waiting for transfers between devices: 35.4 us -> 35.3 us
  transfers between devices with their start and end apart: 5 -> 4, of which waited for: 5 -> 4; matrix products, arithmetic and copies ran while one was open for 0% -> 0% of each run, Pallas kernels for 0% -> 0%
where the time goes in v1:
time: 607 us; the launch traced here: 606 us
  blocking collectives  277 us (46%)
  waiting for transfers between devices  211 us (35%)
  local copies, waits for them, and re-layouts  44.5 us (7%)
  other arithmetic  23.8 us (4%)
  matrix products  19.6 us (3%)
  starting transfers between devices  16 us (3%)
  between operations  14.7 us (2%)
    psum x2, waiting for transfers between devices, gram_sum(): return lax.psum(partial_gram.astype(jnp.bfloat16), 'dp').astype(jnp.float32)  153 us
    all_to_all x1, blocking collectives, per_device(): lax.all_to_all(send_scaled, 'expert', split_axis=0, concat_axis=0, tiled=...  151 us
    all_to_all x1, blocking collectives, per_device(): lax.all_to_all(send_grad, 'expert', split_axis=0, concat_axis=0, tiled=True)  94.8 us
    unnamed x4, waiting for transfers between devices  35.3 us
    all_to_all x1, blocking collectives, per_device(): lax.all_to_all(jnp.stack([scaled_part] * lax.axis_size('dp')), 'dp', 0, 0)  31.3 us
    all_to_all x1, waiting for transfers between devices, per_device(): lax.all_to_all(summed.reshape(experts, capacity, -1).astype(jnp.bfloat16)...  23 us
    scatter x2, local copies, waits for them, and re-layouts, place_slots(): return empty_rows.at[slot_index].set(values)  19.9 us
    another operation x3, other arithmetic  18.2 us
  transfers between devices with their start and end apart: 4, of which 4 were waited for; matrix products, arithmetic and copies ran while one was open for 0% of the time, Pallas kernels for 0%

profile of v1, /device:TPU:2, one launch (start us, length us, event | category | flops | bytes accessed | tf_op | source)
XLA Modules:
  0.0 606.4 jit_solution(2028359757058308746)
XLA Ops:
  7.2 0.8 broadcast_multiply_fusion
  8.0 0.8 copy.27
  9.6 18.0 %reduce-window.6 = s32[64,8,128]{2,1,0:T(8,128)S(1)} reduce-window(s32[64,8,128]{2,1,0:T(8,128)S(1)} %fusion.23, s32[]{:T(128)} %constant.16.clone.1), window={size=1x1x128 pad=0_0x0_0x127_0}, to_apply=%region_0.0 | reduce-window | flops 8323072 | bytes 524292 | tf_op jit(solution)/shard_map/reduce-window
  28.2 12.8 %scatter_custom_fusion = bf16[1280,512]{1,0:T(8,128)(2,1)S(1)} fusion(s32[1024]{0:T(1024)S(1)} %bitcast.54, bf16[512,512]{1,0:T(8,128)(2,1)} %param.5, s32[1024]{0:T(1024)S(1)} %broadcast_clamp_fusion.1, bf16[]{:T(256)} %constant.13.clone.1), kind=kCustom, calls=%fused_computation.24 | custom fusion | bytes 1311232 | tf_op jit(solution)/shard_map/scatter | solution.py:26
  41.0 1.3 reshape.126
  42.3 94.8 %all_to_all.20 = bf16[64,20,512]{2,1,0:T(8,128)(2,1)S(1)} all-to-all(bf16[64,20,512]{2,1,0:T(8,128)(2,1)} %reshape.126), channel_id=1, replica_groups=mesh['dp'=8,'expert'=64] {'expert'}, dimensions={0} | all-to-all | bytes 2621440 | tf_op jit(solution)/shard_map/all_to_all | solution.py:49
  137.1 1.3 reshape.127
  138.4 4.4 convolution_convert_fusion
  142.8 4.4 copy.34
  147.2 35.3 %reduce-scatter.4.cloned.1.call-done = bf16[128,1280]{1,0:T(8,128)(2,1)} async-done(((bf16[1024,1280]{1,0:T(8,128)(2,1)}), bf16[128,1280]{1,0:T(8,128)(2,1)}) %reduce-scatter.4.cloned.1.call-update) | async-done | bytes 327696
  182.5 1.2 copy.35
  183.7 0.8 convert_element_type.61
  184.5 15.7 %all-to-all-start.1 = ((bf16[64,20,128]{2,1,0:T(8,128)(2,1)}), bf16[64,20,128]{2,1,0:T(8,128)(2,1)S(1)}, u32[]{:S(2)}, u32[]{:S(2)}) async-start(bf16[64,20,128]{2,1,0:T(8,128)(2,1)} %convert_element_type.61), calls=%async_computation.1 | async-start | bytes 786432 | tf_op jit(solution)/shard_map/all_to_all | solution.py:65
  200.6 23.0 %all-to-all-done.1 = bf16[64,20,128]{2,1,0:T(8,128)(2,1)S(1)} async-done(((bf16[64,20,128]{2,1,0:T(8,128)(2,1)}), bf16[64,20,128]{2,1,0:T(8,128)(2,1)S(1)}, u32[]{:S(2)}, u32[]{:S(2)}) %all-to-all-start.1) | async-done | bytes 327712 | tf_op jit(solution)/shard_map/all_to_all | solution.py:65
  223.7 2.8 gather_fusion
  226.5 1.4 multiply_convert_fusion.2
  227.9 1.1 stack.2
  229.0 31.3 %all_to_all.21 = bf16[8,512,2,128]{3,2,1,0:T(2,128)(2,1)S(1)} all-to-all(bf16[8,512,2,128]{3,2,1,0:T(2,128)(2,1)S(1)} %stack.2), channel_id=1, replica_groups=mesh['dp'=8,'expert'=64] {'dp'}, dimensions={0} | all-to-all | bytes 4194304 | tf_op jit(solution)/shard_map/all_to_all | solution.py:43
  260.3 2.4 copy.31
  262.7 7.2 %scatter_custom_fusion.1 = bf16[1280,1024]{1,0:T(8,128)(2,1)} fusion(s32[1024]{0:T(1024)S(1)} %bitcast.56, bf16[128,8,8,128]{3,2,1,0:T(8,128)(2,1)S(1)} %bitcast.47, bf16[]{:T(256)} %constant.13.clone.1), kind=kCustom, calls=%fused_computation.11 | custom fusion | bytes 4718594 | tf_op jit(solution)/shard_map/scatter | solution.py:26
  269.9 5.2 reshape.131
  275.1 150.6 %all_to_all.22 = bf16[64,20,1024]{2,1,0:T(8,128)(2,1)S(1)} all-to-all(bf16[64,20,1024]{2,1,0:T(8,128)(2,1)} %reshape.131), channel_id=1, replica_groups=mesh['dp'=8,'expert'=64] {'expert'}, dimensions={0} | all-to-all | bytes 5242880 | tf_op jit(solution)/shard_map/all_to_all | solution.py:50
  425.7 2.9 bitcast_convert_fusion
  428.6 1.0 copy-done.6
  429.5 2.6 convolution_convert_fusion.2
  432.2 71.9 %all-reduce.3.cloned.1.call-done = bf16[1024,1024]{1,0:T(8,128)(2,1)} async-done(((bf16[1024,1024]{1,0:T(8,128)(2,1)}), bf16[1024,1024]{1,0:T(8,128)(2,1)}) %all-reduce.3.cloned.1.call-update) | async-done | bytes 2097168 | tf_op jit(solution)/shard_map/psum | solution.py:21
  504.1 3.4 fusion
  508.2 2.9 subtract_convert_fusion
  511.2 1.0 copy-done.7
  512.2 2.6 convolution_convert_fusion.1
  514.8 80.9 %all-reduce.5.cloned.1.call-done = bf16[1024,1024]{1,0:T(8,128)(2,1)} async-done(((bf16[1024,1024]{1,0:T(8,128)(2,1)}), bf16[1024,1024]{1,0:T(8,128)(2,1)}) %all-reduce.5.cloned.1.call-update) | async-done | bytes 2097168 | tf_op jit(solution)/shard_map/psum | solution.py:21
  595.7 4.2 multiply_bitcast_fusion
  (40 shorter events, 1.9 us)
Async XLA Ops:
  7.2 131.2 %copy-start = (bf16[1,1024,512]{2,1,0:T(8,128)(2,1)S(1)}, bf16[1,1024,512]{2,1,0:T(8,128)(2,1)}, u32[]{:S(2)}) copy-start(bf16[1,1024,512]{2,1,0:T(8,128)(2,1)} %param.9) | copy-start | bytes 3145732
  7.2 175.3 %reduce-scatter.4.cloned.1.call-start = ((), (), s32[]{:S(2)}) async-start(), calls=%async_computation.7 | async-start | bytes 2949120
  137.1 5.7 copy-start.1
  147.2 53.2 %copy-start.5 = (f32[512,2]{0,1:T(2,128)S(1)}, f32[512,2]{0,1:T(2,128)}, u32[]{:S(2)}) copy-start(f32[512,2]{0,1:T(2,128)} %param.7) | copy-start | bytes 12292
  184.5 39.1 %all-to-all-start.1 = ((bf16[64,20,128]{2,1,0:T(8,128)(2,1)}), bf16[64,20,128]{2,1,0:T(8,128)(2,1)S(1)}, u32[]{:S(2)}, u32[]{:S(2)}) async-start(bf16[64,20,128]{2,1,0:T(8,128)(2,1)} %convert_element_type.61), calls=%async_computation.1 | async-start | bytes 786432 | tf_op jit(solution)/shard_map/all_to_all | solution.py:65
  200.2 303.9 %all-reduce.3.cloned.1.call-start = ((), (), s32[]{:S(2)}) async-start(), calls=%async_computation.5 | async-start | bytes 4194304 | tf_op jit(solution)/shard_map/psum | solution.py:21
  223.7 2.8 copy-start.4
  275.1 150.6 %copy-start.2 = (bf16[64,20,512]{2,1,0:T(8,128)(2,1)S(1)}, bf16[64,20,512]{2,1,0:T(8,128)(2,1)}, u32[]{:S(2)}) copy-start(bf16[64,20,512]{2,1,0:T(8,128)(2,1)} %copy-done.1) | copy-start | bytes 3932164
  428.6 1.0 copy-start.6
  432.2 163.5 %all-reduce.5.cloned.1.call-start = ((), (), s32[]{:S(2)}) async-start(), calls=%async_computation.6 | async-start | bytes 4194304 | tf_op jit(solution)/shard_map/psum | solution.py:21
  504.1 4.2 copy-start.3
  511.2 1.0 copy-start.7
  514.8 80.9 %copy-start.8 = (bf16[1024,512]{1,0:T(8,128)(2,1)S(1)}, bf16[1024,512]{1,0:T(8,128)(2,1)}, u32[]{:S(2)}) copy-start(bf16[1024,512]{1,0:T(8,128)(2,1)} %copy-done.7) | copy-start | bytes 3145732
Sparse Core Ops, SparseCore 0:
  147.3 35.1 reduce-scatter.3
  432.3 71.7 all-reduce.2
  514.9 80.6 all-reduce.4
